TPU v7x, 512 devices: a whole 4x4x16 slice. The times are simulated.
512 devices in a mesh: dp: 4 (over y), expert: 32 (over z, core), tensor: 4 (over x).
Axes of the slice: x: 4, y: 4, z: 16, core: 2. Of those that a mesh axis runs over, the one named last changes fastest.
Arguments:
- tokens: bfloat16 [16384, 2048], P(('dp', 'expert')), may hold values from -6 to 6
- cotangent: bfloat16 [16384, 2048], P(('dp', 'expert')), may hold values from -6 to 6
- expert_ids: int32 [16384, 1], P(('dp', 'expert')), may hold values from 0 to 31; in each aligned block of 128 rows (0 to 127, 128 to 255, ...) at most 8 rows name the same one
- gate_weight: bfloat16 [32, 2048, 1408], P('expert', 'dp', 'tensor'), may hold values from -0.125 to 0.125
- up_weight: bfloat16 [32, 2048, 1408], P('expert', 'dp', 'tensor'), may hold values from -0.125 to 0.125
- down_weight: bfloat16 [32, 2048, 1408], P('expert', 'dp', 'tensor'), may hold values from -0.15625 to 0.15625
Outputs:
- grad_tokens: bfloat16 [16384, 2048], P(('dp', 'expert'), 'tensor')
- grad_gate: bfloat16 [32, 2048, 1408], P('expert', 'dp', 'tensor')
- grad_up: bfloat16 [32, 2048, 1408], P('expert', 'dp', 'tensor')
Inputs may be any that keep to these rules, and one draw needn't show every extreme that they name: `expert_ids`: among the 128 tokens of one block no expert id occurs more than 8 times, and in every draw some block holds some id exactly 8 times.
All inputs are finite; a program needn't handle non-finite values.
Results may differ from a plain program's by a relative error of at most 0.013.
Values may be sent and summed in bfloat16 or wider, within the bound.
A program may use at most 64 MiB of HBM per device.

v0:
```python
import jax
import jax.numpy as jnp
from jax import lax
from jax.sharding import PartitionSpec as P

CAP = 8


def bucket_matrix(expert_ids, expert_count, capacity):
    chosen = expert_ids[:, 0]
    columns = jnp.arange(expert_count, dtype=jnp.int32)
    onehot = (chosen[:, None] == columns[None, :]).astype(jnp.int32)
    earlier = jnp.cumsum(onehot, axis=0) - onehot
    position = jnp.sum(earlier * onehot, axis=1)
    target = chosen * capacity + position
    slot_rows = jnp.arange(expert_count * capacity, dtype=jnp.int32)
    return (slot_rows[:, None] == target[None, :]).astype(jnp.bfloat16)


def on_device(tokens, cotangent, expert_ids, gate_weight, up_weight, down_weight):
    owners = lax.axis_size("expert")
    feature_count = tokens.shape[1]
    local_experts = gate_weight.shape[0]
    expert_count = local_experts * owners
    slot_count = owners * CAP
    placer = bucket_matrix(expert_ids, expert_count, CAP)
    gate_full, up_full, down_full = (
        lax.all_gather(gate_weight, "dp", axis=1, tiled=True),
        lax.all_gather(up_weight, "dp", axis=1, tiled=True),
        lax.all_gather(down_weight, "dp", axis=1, tiled=True),
    )

    def to_buckets(rows):
        packed = jnp.dot(placer, rows, preferred_element_type=jnp.float32).astype(jnp.bfloat16)
        return packed.reshape(owners, local_experts, CAP, rows.shape[1])

    arrived_tokens, arrived_grads = (
        lax.all_to_all(to_buckets(tokens), "expert", split_axis=0, concat_axis=2, tiled=True),
        lax.all_to_all(to_buckets(cotangent), "expert", split_axis=0, concat_axis=2, tiled=True),
    )
    inputs = arrived_tokens.reshape(local_experts, slot_count, feature_count)
    grads_in = arrived_grads.reshape(local_experts, slot_count, feature_count)
    gate_act = jnp.einsum("esd,edf->esf", inputs, gate_full, preferred_element_type=jnp.float32)
    up_act = jnp.einsum("esd,edf->esf", inputs, up_full, preferred_element_type=jnp.float32)
    hidden_grad = jnp.einsum(
        "esd,edf->esf", grads_in, down_full, preferred_element_type=jnp.float32
    )
    sigmoid_gate = jax.nn.sigmoid(gate_act)
    up_grad = (hidden_grad * gate_act * sigmoid_gate).astype(jnp.bfloat16)
    gate_grad = (
        hidden_grad * up_act * sigmoid_gate * (1.0 + gate_act * (1.0 - sigmoid_gate))
    ).astype(jnp.bfloat16)
    partial_value = jnp.einsum(
        "esf,edf->esd", gate_grad, gate_full, preferred_element_type=jnp.float32
    )
    partial_value = partial_value + jnp.einsum(
        "esf,edf->esd", up_grad, up_full, preferred_element_type=jnp.float32
    )
    gate_term = jnp.einsum("esd,esf->edf", inputs, gate_grad, preferred_element_type=jnp.float32)
    up_term = jnp.einsum("esd,esf->edf", inputs, up_grad, preferred_element_type=jnp.float32)
    grad_gate, grad_up = (
        lax.psum_scatter(
            gate_term.astype(jnp.bfloat16), "dp", scatter_dimension=1, tiled=True
        ).astype(jnp.float32),
        lax.psum_scatter(
            up_term.astype(jnp.bfloat16), "dp", scatter_dimension=1, tiled=True
        ).astype(jnp.float32),
    )
    contract = (((0,), (0,)), ((), ()))
    outgoing_back = partial_value.astype(jnp.bfloat16).reshape(
        1, local_experts, slot_count, feature_count
    )
    returned = lax.all_to_all(outgoing_back, "expert", split_axis=2, concat_axis=0, tiled=True)
    flat_rows = returned.reshape(expert_count * CAP, feature_count)
    per_token = lax.dot_general(placer, flat_rows, contract, preferred_element_type=jnp.float32)
    summed = lax.psum_scatter(
        per_token.astype(jnp.bfloat16), "tensor", scatter_dimension=1, tiled=True
    )
    return (summed, grad_gate.astype(jnp.bfloat16), grad_up.astype(jnp.bfloat16))


def solution(mesh):
    placed = (
        P(("dp", "expert"), None),
        P(("dp", "expert"), None),
        P(("dp", "expert"), None),
        P("expert", "dp", "tensor"),
        P("expert", "dp", "tensor"),
        P("expert", "dp", "tensor"),
    )
    return jax.shard_map(
        on_device,
        mesh=mesh,
        in_specs=placed,
        out_specs=(
            P(("dp", "expert"), "tensor"),
            P("expert", "dp", "tensor"),
            P("expert", "dp", "tensor"),
        ),
        check_vma=False,
    )
```

profile of v0, /device:TPU:1, one launch (start us, length us, event | category | flops | bytes accessed | tf_op | source)
XLA Modules:
  0.0 280.2 jit_solution(13116984333326666507)
XLA Ops:
  7.2 0.8 fusion.37
  8.2 0.8 select_reduce_fusion
  9.0 0.7 multiply_add_fusion
  9.7 1.4 fusion.5
  11.1 16.9 %all-to-all-start.1 = ((bf16[32,1,8,2048]{3,2,1,0:T(8,128)(2,1)}), bf16[32,1,8,2048]{3,2,1,0:T(8,128)(2,1)S(1)}, u32[]{:S(2)}, u32[]{:S(2)}) async-start(bf16[32,1,8,2048]{3,2,1,0:T(8,128)(2,1)} %fusion.5), calls=%async_computation.1 | async-start | bytes 2097152 | tf_op jit(solution)/shard_map/all_to_all | solution.py:38
  28.0 0.7 all-gather.8.cloned.1.call-update
  28.7 1.4 fusion.4
  30.1 53.6 %all-to-all-done.1 = bf16[32,1,8,2048]{3,2,1,0:T(8,128)(2,1)S(1)} async-done(((bf16[32,1,8,2048]{3,2,1,0:T(8,128)(2,1)}), bf16[32,1,8,2048]{3,2,1,0:T(8,128)(2,1)S(1)}, u32[]{:S(2)}, u32[]{:S(2)}) %all-to-all-start.1) | async-done | bytes 1048608 | tf_op jit(solution)/shard_map/all_to_all | solution.py:38
  83.7 4.1 %all-to-all-start = ((bf16[32,1,8,2048]{3,2,1,0:T(8,128)(2,1)}), bf16[32,1,8,2048]{3,2,1,0:T(8,128)(2,1)S(1)}, u32[]{:S(2)}, u32[]{:S(2)}) async-start(bf16[32,1,8,2048]{3,2,1,0:T(8,128)(2,1)} %fusion.4), calls=%async_computation | async-start | bytes 2097152 | tf_op jit(solution)/shard_map/all_to_all | solution.py:39
  87.8 0.7 all-gather.4.cloned.1.call-update
  88.6 0.7 all-gather.6.cloned.1.call-update
  89.2 0.2 reduce-scatter.6.cloned.1.call-start
  89.5 1.9 fusion.8
  91.4 33.1 %all-gather.4.cloned.1.call-done = bf16[1,2048,352]{1,2,0:T(8,128)(2,1)} async-done(((bf16[1,512,352]{1,2,0:T(8,128)(2,1)}), bf16[1,2048,352]{1,2,0:T(8,128)(2,1)}) %all-gather.4.cloned.1.call-update) | async-done | bytes 1441808 | tf_op jit(solution)/shard_map/all_gather | solution.py:30
  124.5 19.1 %all-to-all-done = bf16[32,1,8,2048]{3,2,1,0:T(8,128)(2,1)S(1)} async-done(((bf16[32,1,8,2048]{3,2,1,0:T(8,128)(2,1)}), bf16[32,1,8,2048]{3,2,1,0:T(8,128)(2,1)S(1)}, u32[]{:S(2)}, u32[]{:S(2)}) %all-to-all-start) | async-done | bytes 1048608 | tf_op jit(solution)/shard_map/all_to_all | solution.py:39
  143.6 2.7 multiply_convert_fusion
  146.3 14.1 %all-gather.6.cloned.1.call-done = bf16[1,2048,352]{1,2,0:T(8,128)(2,1)} async-done(((bf16[1,512,352]{1,2,0:T(8,128)(2,1)}), bf16[1,2048,352]{1,2,0:T(8,128)(2,1)}) %all-gather.6.cloned.1.call-update) | async-done | bytes 1441808 | tf_op jit(solution)/shard_map/all_gather | solution.py:29
  160.4 2.0 fusion.24
  162.4 1.7 fusion.1
  164.1 0.7 fusion.6
  164.8 0.6 copy-done.2
  165.5 0.7 fusion.3
  166.2 2.9 %copy.21 = bf16[1,1,256,2048]{3,1,0,2:T(2,128)(2,1)} copy(bf16[1,1,256,2048]{3,2,1,0:T(8,128)(2,1)S(1)} %fusion.3) | data formatting | bytes 2097152 | tf_op jit(solution)/shard_map/reshape | solution.py:70
  169.1 0.5 broadcast.19
  169.6 8.0 %reduce = bf16[256,2048]{1,0:T(8,128)(2,1)S(1)} reduce(bf16[256,1,1,2048]{3,2,1,0:T(2,128)(2,1)} %bitcast.66, bf16[]{:T(256)} %broadcast.19), dimensions={1,2}, to_apply=%bitcast.65.reduce_sub_computation | reduce | bytes 2097154
  177.7 1.9 reshape.108
  179.6 13.2 %all-to-all-start.2 = ((bf16[32,2,8192]{2,1,0:T(2,128)(2,1)}), bf16[32,2,8192]{2,1,0:T(2,128)(2,1)S(1)}, u32[]{:S(2)}, u32[]{:S(2)}) async-start(bf16[32,2,8192]{2,1,0:T(2,128)(2,1)} %reshape.108), calls=%async_computation.2 | async-start | bytes 2097152 | tf_op jit(solution)/shard_map/all_to_all | solution.py:73
  192.9 1.7 fusion.2
  194.6 53.9 %all-to-all-done.2 = bf16[32,2,8192]{2,1,0:T(2,128)(2,1)S(1)} async-done(((bf16[32,2,8192]{2,1,0:T(2,128)(2,1)}), bf16[32,2,8192]{2,1,0:T(2,128)(2,1)S(1)}, u32[]{:S(2)}, u32[]{:S(2)}) %all-to-all-start.2) | async-done | bytes 1048608 | tf_op jit(solution)/shard_map/all_to_all | solution.py:73
  248.5 3.5 %reshape.109 = bf16[256,1,1,2048]{3,2,1,0:T(2,128)(2,1)} reshape(bf16[32,2,8192]{2,1,0:T(2,128)(2,1)S(1)} %all-to-all-done.2) | data formatting | bytes 2097152
  252.0 3.1 %convolution_convert_fusion.4 = bf16[128,2048]{1,0:T(8,128)(2,1)} fusion(bf16[1,1,256,2048]{3,1,0,2:T(2,128)(2,1)} %bitcast.67, s32[128]{0:T(128)S(1)} %multiply_add_fusion), kind=kOutput, calls=%fused_computation.11 | convolution fusion | flops 134512640 | bytes 1573376 | tf_op jit(solution)/shard_map/dot_general | solution.py:75
  255.2 18.2 %reduce-scatter.4.cloned.1.call-done = bf16[128,512]{1,0:T(8,128)(2,1)} async-done(((bf16[128,2048]{1,0:T(8,128)(2,1)}), bf16[128,512]{1,0:T(8,128)(2,1)}) %reduce-scatter.4.cloned.1.call-update) | async-done | bytes 131088 | tf_op jit(solution)/shard_map/reduce_scatter | solution.py:76
  (19 shorter events, 0.5 us)
Async XLA Ops:
  7.2 2.5 copy-start
  11.1 17.6 %copy-start.3 = (bf16[128,2048]{1,0:T(8,128)(2,1)S(1)}, bf16[128,2048]{1,0:T(8,128)(2,1)}, u32[]{:S(2)}) copy-start(bf16[128,2048]{1,0:T(8,128)(2,1)} %param.7) | copy-start | bytes 1572868
  11.1 72.6 %all-to-all-start.1 = ((bf16[32,1,8,2048]{3,2,1,0:T(8,128)(2,1)}), bf16[32,1,8,2048]{3,2,1,0:T(8,128)(2,1)S(1)}, u32[]{:S(2)}, u32[]{:S(2)}) async-start(bf16[32,1,8,2048]{3,2,1,0:T(8,128)(2,1)} %fusion.5), calls=%async_computation.1 | async-start | bytes 2097152 | tf_op jit(solution)/shard_map/all_to_all | solution.py:38
  27.9 61.5 %all-gather.8.cloned.1.call-start = ((), (), s32[]{:S(2)}) async-start(), calls=%async_computation.8 | async-start | bytes 1802240 | tf_op jit(solution)/shard_map/all_gather | solution.py:28
  83.7 59.9 %all-to-all-start = ((bf16[32,1,8,2048]{3,2,1,0:T(8,128)(2,1)}), bf16[32,1,8,2048]{3,2,1,0:T(8,128)(2,1)S(1)}, u32[]{:S(2)}, u32[]{:S(2)}) async-start(bf16[32,1,8,2048]{3,2,1,0:T(8,128)(2,1)} %fusion.4), calls=%async_computation | async-start | bytes 2097152 | tf_op jit(solution)/shard_map/all_to_all | solution.py:39
  87.8 36.7 %all-gather.4.cloned.1.call-start = ((), (), s32[]{:S(2)}) async-start(), calls=%async_computation.6 | async-start | bytes 1802240 | tf_op jit(solution)/shard_map/all_gather | solution.py:30
  88.5 71.9 %all-gather.6.cloned.1.call-start = ((), (), s32[]{:S(2)}) async-start(), calls=%async_computation.7 | async-start | bytes 1802240 | tf_op jit(solution)/shard_map/all_gather | solution.py:29
  89.2 165.9 %reduce-scatter.6.cloned.1.call-start = ((), (), s32[]{:S(2)}) async-start(), calls=%async_computation.10 | async-start | bytes 1802240 | tf_op jit(solution)/shard_map/reduce_scatter | solution.py:62
  162.4 1.7 copy-start.1
  164.1 1.4 copy-start.2
  179.6 69.0 %all-to-all-start.2 = ((bf16[32,2,8192]{2,1,0:T(2,128)(2,1)}), bf16[32,2,8192]{2,1,0:T(2,128)(2,1)S(1)}, u32[]{:S(2)}, u32[]{:S(2)}) async-start(bf16[32,2,8192]{2,1,0:T(2,128)(2,1)} %reshape.108), calls=%async_computation.2 | async-start | bytes 2097152 | tf_op jit(solution)/shard_map/all_to_all | solution.py:73
  192.8 62.4 %reduce-scatter.8.cloned.1.call-start = ((), (), s32[]{:S(2)}) async-start(), calls=%async_computation.11 | async-start | bytes 1802240 | tf_op jit(solution)/shard_map/reduce_scatter | solution.py:65
  194.5 78.8 %reduce-scatter.4.cloned.1.call-start = ((), (), s32[]{:S(2)}) async-start(), calls=%async_computation.9 | async-start | bytes 655360 | tf_op jit(solution)/shard_map/reduce_scatter | solution.py:76
Sparse Core Ops, SparseCore 0:
  30.9 33.6 all-gather.7
  90.7 33.7 all-gather.3
  126.6 33.7 all-gather.5
  164.2 32.0 reduce-scatter.5
  199.6 32.6 reduce-scatter.7
  255.3 18.0 reduce-scatter.3
where the time goes:
time: 282 us; the launch traced here: 280 us
  waiting for transfers between devices  194 us (69%)
  starting transfers between devices  34.6 us (12%)
  matrix products  17.4 us (6%)
  between operations  14.2 us (5%)
  other arithmetic  10.5 us (4%)
  local copies, waits for them, and re-layouts  9.44 us (3%)
    all_to_all x1, waiting for transfers between devices, on_device(): lax.all_to_all(outgoing_back, 'expert', split_axis=2, concat_axis=0, tile...  53.9 us
    all_to_all x1, waiting for transfers between devices, on_device(): lax.all_to_all(to_buckets(tokens), 'expert', split_axis=0, concat_axis=2,...  53.6 us
    all_gather x1, waiting for transfers between devices, on_device(): lax.all_gather(down_weight, 'dp', axis=1, tiled=True)  33.1 us
    all_to_all x1, waiting for transfers between devices, on_device(): lax.all_to_all(to_buckets(cotangent), 'expert', split_axis=0, concat_axis...  19.1 us
    reduce_scatter x1, waiting for transfers between devices, on_device(): lax.psum_scatter(per_token.astype(jnp.bfloat16), 'tensor', scatter_dimens...  18.2 us
    all_to_all x1, starting transfers between devices, on_device(): lax.all_to_all(to_buckets(tokens), 'expert', split_axis=0, concat_axis=2,...  16.9 us
    all_gather x1, waiting for transfers between devices, on_device(): lax.all_gather(up_weight, 'dp', axis=1, tiled=True)  14.1 us
    all_to_all x1, starting transfers between devices, on_device(): lax.all_to_all(outgoing_back, 'expert', split_axis=2, concat_axis=0, tile...  13.2 us
  transfers between devices with their start and end apart: 9, of which 6 were waited for; matrix products, arithmetic and copies ran while one was open for 10% of the time, Pallas kernels for 0%

commit v1 on v0

v1 whole, which is shorter than its diff:
```python
import jax
import jax.numpy as jnp
from jax import lax
from jax.sharding import PartitionSpec as P

CAP = 8


def bucket_matrix(expert_ids, expert_count, capacity):
    chosen = expert_ids[:, 0]
    columns = jnp.arange(expert_count, dtype=jnp.int32)
    onehot = (chosen[:, None] == columns[None, :]).astype(jnp.int32)
    earlier = jnp.cumsum(onehot, axis=0) - onehot
    position = jnp.sum(earlier * onehot, axis=1)
    target = chosen * capacity + position
    slot_rows = jnp.arange(expert_count * capacity, dtype=jnp.int32)
    return (slot_rows[:, None] == target[None, :]).astype(jnp.bfloat16)


def on_device(tokens, cotangent, expert_ids, gate_weight, up_weight, down_weight):
    owners = lax.axis_size("expert")
    shards = lax.axis_size("tensor")
    features = tokens.shape[1]
    part = features // shards
    local_experts = gate_weight.shape[0]
    expert_count = local_experts * owners
    slot_count = owners * CAP
    placer = bucket_matrix(expert_ids, expert_count, CAP)
    gate_full, down_full, up_full = (
        lax.all_gather(w, "dp", axis=1, tiled=True)[0] for w in (gate_weight, down_weight, up_weight)
    )
    start = lax.axis_index("tensor") * part
    mine = jnp.concatenate(
        [lax.dynamic_slice_in_dim(a, start, part, axis=1) for a in (tokens, cotangent)], axis=1
    )
    packed = jnp.dot(placer, mine, preferred_element_type=jnp.float32).astype(jnp.bfloat16)
    arrived = lax.all_to_all(
        packed.reshape(owners, CAP, 2 * part), "expert", split_axis=0, concat_axis=0, tiled=True
    ).reshape(slot_count, 2 * part)
    whole = lax.all_gather(arrived, "tensor", axis=0, tiled=False)
    inputs = jnp.concatenate([whole[t, :, :part] for t in range(shards)], axis=1)
    grads_in = jnp.concatenate([whole[t, :, part:] for t in range(shards)], axis=1)
    gate_act = jnp.dot(inputs, gate_full, preferred_element_type=jnp.float32)
    hidden_grad = jnp.dot(grads_in, down_full, preferred_element_type=jnp.float32)
    up_act = jnp.dot(inputs, up_full, preferred_element_type=jnp.float32)
    sigmoid_gate = jax.nn.sigmoid(gate_act)
    up_grad = (hidden_grad * gate_act * sigmoid_gate).astype(jnp.bfloat16)
    gate_grad = (
        hidden_grad * up_act * sigmoid_gate * (1.0 + gate_act * (1.0 - sigmoid_gate))
    ).astype(jnp.bfloat16)
    contract = (((1,), (1,)), ((), ()))
    partial_value = lax.dot_general(gate_grad, gate_full, contract, preferred_element_type=jnp.float32)
    partial_value = partial_value + lax.dot_general(
        up_grad, up_full, contract, preferred_element_type=jnp.float32
    )
    rows = (((0,), (0,)), ((), ()))
    gate_term = lax.dot_general(inputs, gate_grad, rows, preferred_element_type=jnp.float32)
    up_term = lax.dot_general(inputs, up_grad, rows, preferred_element_type=jnp.float32)
    summed = lax.psum_scatter(
        partial_value.astype(jnp.bfloat16), "tensor", scatter_dimension=1, tiled=True
    )
    grad_gate, grad_up = (
        lax.psum_scatter(term.astype(jnp.bfloat16), "dp", scatter_dimension=0, tiled=True)[None]
        for term in (gate_term, up_term)
    )
    returned = lax.all_to_all(
        summed.reshape(owners, CAP, part), "expert", split_axis=0, concat_axis=0, tiled=True
    ).reshape(slot_count, part)
    per_token = lax.dot_general(placer, returned, rows, preferred_element_type=jnp.float32)
    return (per_token.astype(jnp.bfloat16), grad_gate, grad_up)


def solution(mesh):
    placed = (
        P(("dp", "expert"), None),
        P(("dp", "expert"), None),
        P(("dp", "expert"), None),
        P("expert", "dp", "tensor"),
        P("expert", "dp", "tensor"),
        P("expert", "dp", "tensor"),
    )
    return jax.shard_map(
        on_device,
        mesh=mesh,
        in_specs=placed,
        out_specs=(
            P(("dp", "expert"), "tensor"),
            P("expert", "dp", "tensor"),
            P("expert", "dp", "tensor"),
        ),
        check_vma=False,
    )
```

time: 282 us -> 314 us (1.11)
  blocking collectives: 0 us -> 86.6 us
  starting transfers between devices: 34.6 us -> 0.28 us
  other arithmetic: 10.5 us -> 2.4 us
  local copies, waits for them, and re-layouts: 9.44 us -> 3.33 us
  matrix products: 17.4 us -> 12.9 us
    all_to_all x3 -> x0, waiting for transfers between devices: 127 us -> none  [the longest x1 53.9 us: on_device(): lax.all_to_all(outgoing_back, 'expert', split_axis=2, concat_axis=0, tile...]
    all_to_all x0 -> x2, blocking collectives: none -> 86.6 us  [the longest x1 50.2 us: on_device(): lax.all_to_all(packed.reshape(owners, CAP, 2 * part), 'expert', split_axi...]
    all_gather x3 -> x4, waiting for transfers between devices: 47.1 us -> 129 us  [the longest x3 101 us: on_device(): lax.all_gather(w, 'dp', axis=1, tiled=True)[0]]
    reduce_scatter x3, waiting for transfers between devices: 18.2 us -> 62.3 us  [the longest x2 35 us: on_device(): lax.psum_scatter(term.astype(jnp.bfloat16), 'dp', scatter_dimension=0, ti...]
    all_to_all x3 -> x0, starting transfers between devices: 34.2 us -> none  [the longest x1 16.9 us: on_device(): lax.all_to_all(to_buckets(tokens), 'expert', split_axis=0, concat_axis=2,...]
    unnamed x1 -> x0, other arithmetic: 8.03 us -> none
    unnamed x11 -> x4, local copies, waits for them, and re-layouts: 6.51 us -> 0.63 us
    dot_general x10 -> x9, matrix products: 17.4 us -> 12.9 us  [the longest x1 2.07 us: on_device(): up_act = jnp.dot(inputs, up_full, preferred_element_type=jnp.float32)]
  transfers between devices with their start and end apart: 9 -> 7, of which waited for: 6 -> 6; matrix products, arithmetic and copies ran while one was open for 10% -> 3% of each run, Pallas kernels for 0% -> 0%
where the time goes in v1:
time: 314 us; the launch traced here: 313 us
  waiting for transfers between devices  193 us (61%)
  blocking collectives  86.6 us (28%)
  between operations  14.2 us (5%)
  matrix products  12.9 us (4%)
  local copies, waits for them, and re-layouts  3.33 us (1%)
    all_gather x3, waiting for transfers between devices, on_device(): lax.all_gather(w, 'dp', axis=1, tiled=True)[0]  101 us
    all_to_all x1, blocking collectives, on_device(): lax.all_to_all(packed.reshape(owners, CAP, 2 * part), 'expert', split_axi...  50.2 us
    all_to_all x1, blocking collectives, on_device(): lax.all_to_all(summed.reshape(owners, CAP, part), 'expert', split_axis=0,...  36.4 us
    reduce_scatter x2, waiting for transfers between devices, on_device(): lax.psum_scatter(term.astype(jnp.bfloat16), 'dp', scatter_dimension=0, ti...  35 us
    all_gather x1, waiting for transfers between devices, on_device(): whole = lax.all_gather(arrived, 'tensor', axis=0, tiled=False)  27.9 us
    reduce_scatter x1, waiting for transfers between devices, on_device(): lax.psum_scatter(partial_value.astype(jnp.bfloat16), 'tensor', scatter_di...  27.3 us
  transfers between devices with their start and end apart: 7, of which 6 were waited for; matrix products, arithmetic and copies ran while one was open for 3% of the time, Pallas kernels for 0%

profile of v1, /device:TPU:1, one launch (start us, length us, event | category | flops | bytes accessed | tf_op | source)
XLA Modules:
  0.0 313.0 jit_solution(8685269563842167810)
XLA Ops:
  7.2 0.0 all-gather.5.cloned.1.call-start
  7.2 0.7 fusion.36
  8.0 0.2 reduce_window_sum.11
  8.1 0.8 select_reduce_fusion
  9.0 0.7 multiply_add_fusion
  9.6 1.0 constant_dynamic-slice_fusion
  10.6 0.3 fusion.10
  10.9 50.2 %all_to_all.10 = bf16[32,8,1024]{2,1,0:T(8,128)(2,1)} all-to-all(bf16[32,8,1024]{2,1,0:T(8,128)(2,1)S(1)} %fusion.10), channel_id=1, replica_groups=mesh['dp'=4,'expert'=32,'tensor'=4] {'expert'}, dimensions={0} | all-to-all | bytes 1048576 | tf_op jit(solution)/shard_map/all_to_all | solution.py:37
  61.1 0.0 all-gather.11.cloned.1.call-start
  61.1 0.7 all-gather.11.cloned.1.call-update
  61.9 0.7 all-gather.7.cloned.1.call-update
  62.6 0.5 all-gather.9.cloned.1.call-update
  63.2 0.0 reduce-scatter.4.cloned.1.call-start
  63.2 27.9 %all-gather.5.cloned.1.call-done = bf16[4,256,1024]{2,1,0:T(8,128)(2,1)} async-done(((bf16[1,256,1024]{2,1,0:T(8,128)(2,1)}), bf16[4,256,1024]{2,1,0:T(8,128)(2,1)}) %all-gather.5.cloned.1.call-update) | async-done | bytes 2097168 | tf_op jit(solution)/shard_map/all_gather | solution.py:40
  91.1 1.7 slice_bitcast_fusion.3
  92.8 33.4 %all-gather.11.cloned.1.call-done = bf16[1,2048,352]{1,2,0:T(8,128)(2,1)} async-done(((bf16[1,512,352]{1,2,0:T(8,128)(2,1)}), bf16[1,2048,352]{1,2,0:T(8,128)(2,1)}) %all-gather.11.cloned.1.call-update) | async-done | bytes 1441808 | tf_op jit(solution)/shard_map/all_gather | solution.py:30
  126.3 1.9 fusion.3
  128.2 33.9 %all-gather.7.cloned.1.call-done = bf16[1,2048,352]{1,2,0:T(8,128)(2,1)} async-done(((bf16[1,512,352]{1,2,0:T(8,128)(2,1)}), bf16[1,2048,352]{1,2,0:T(8,128)(2,1)}) %all-gather.7.cloned.1.call-update) | async-done | bytes 1441808 | tf_op jit(solution)/shard_map/all_gather | solution.py:30
  162.1 2.0 multiply_convert_fusion
  164.1 33.8 %all-gather.9.cloned.1.call-done = bf16[1,2048,352]{1,2,0:T(8,128)(2,1)} async-done(((bf16[1,512,352]{1,2,0:T(8,128)(2,1)}), bf16[1,2048,352]{1,2,0:T(8,128)(2,1)}) %all-gather.9.cloned.1.call-update) | async-done | bytes 1441808 | tf_op jit(solution)/shard_map/all_gather | solution.py:30
  197.9 2.1 fusion.20
  200.0 0.7 fusion.1
  200.7 0.6 copy-done.1
  201.3 1.7 fusion
  203.1 0.0 reduce-scatter.8.cloned.1.call-start
  203.1 1.6 convolution_convert_fusion
  204.8 0.0 reduce-scatter.6.cloned.1.call-start
  204.8 1.7 convolution_convert_fusion.1
  206.5 27.3 %reduce-scatter.4.cloned.1.call-done = bf16[256,512]{1,0:T(8,128)(2,1)} async-done(((bf16[256,2048]{1,0:T(8,128)(2,1)}), bf16[256,512]{1,0:T(8,128)(2,1)}) %reduce-scatter.4.cloned.1.call-update) | async-done | bytes 262160 | tf_op jit(solution)/shard_map/reduce_scatter | solution.py:59
  233.8 36.4 %all_to_all.11 = bf16[32,8,512]{2,1,0:T(8,128)(2,1)S(1)} all-to-all(bf16[32,8,512]{2,1,0:T(8,128)(2,1)} %bitcast.55), channel_id=1, replica_groups=mesh['dp'=4,'expert'=32,'tensor'=4] {'expert'}, dimensions={0} | all-to-all | bytes 524288 | tf_op jit(solution)/shard_map/all_to_all | solution.py:66
  270.2 0.9 convolution_convert_fusion.3
  271.1 35.0 %reduce-scatter.6.cloned.1.call-done = bf16[512,352]{0,1:T(8,128)(2,1)} async-done(((bf16[2048,352]{0,1:T(8,128)(2,1)}), bf16[512,352]{0,1:T(8,128)(2,1)}) %reduce-scatter.6.cloned.1.call-update) | async-done | bytes 360464 | tf_op jit(solution)/shard_map/reduce_scatter | solution.py:63
  (10 shorter events, 0.1 us)
Async XLA Ops:
  7.2 83.9 %all-gather.5.cloned.1.call-start = ((), (), s32[]{:S(2)}) async-start(), calls=%async_computation.5 | async-start | bytes 2621440 | tf_op jit(solution)/shard_map/all_gather | solution.py:40
  61.1 65.2 %all-gather.11.cloned.1.call-start = ((), (), s32[]{:S(2)}) async-start(), calls=%async_computation.8 | async-start | bytes 1802240 | tf_op jit(solution)/shard_map/all_gather | solution.py:30
  61.8 100.3 %all-gather.7.cloned.1.call-start = ((), (), s32[]{:S(2)}) async-start(), calls=%async_computation.6 | async-start | bytes 1802240 | tf_op jit(solution)/shard_map/all_gather | solution.py:30
  62.6 135.3 %all-gather.9.cloned.1.call-start = ((), (), s32[]{:S(2)}) async-start(), calls=%async_computation.7 | async-start | bytes 1802240 | tf_op jit(solution)/shard_map/all_gather | solution.py:30
  63.2 170.7 %reduce-scatter.4.cloned.1.call-start = ((), (), s32[]{:S(2)}) async-start(), calls=%async_computation.9 | async-start | bytes 1310720 | tf_op jit(solution)/shard_map/reduce_scatter | solution.py:59
  197.9 2.1 copy-start
  200.0 1.4 copy-start.1
  203.1 68.1 %reduce-scatter.8.cloned.1.call-start = ((), (), s32[]{:S(2)}) async-start(), calls=%async_computation.11 | async-start | bytes 1802240 | tf_op jit(solution)/shard_map/reduce_scatter | solution.py:63
  204.8 101.3 %reduce-scatter.6.cloned.1.call-start = ((), (), s32[]{:S(2)}) async-start(), calls=%async_computation.10 | async-start | bytes 1802240 | tf_op jit(solution)/shard_map/reduce_scatter | solution.py:63
Sparse Core Ops, SparseCore 0:
  61.2 29.8 all-gather.4
  93.2 33.0 all-gather.10
  128.4 33.7 all-gather.6
  164.1 33.7 all-gather.8
  203.2 30.6 reduce-scatter.3
  237.4 32.6 reduce-scatter.7
  273.7 32.3 reduce-scatter.5
